TPU v7x, 32 devices: a whole 2x2x4 slice. The times are simulated.
32 devices in a mesh: groups: 2 (over x), seq: 16 (over z, y, core).
Axes of the slice: x: 2, y: 2, z: 4, core: 2. Of those that a mesh axis runs over, the one named last changes fastest.
Arguments:
- visual: bfloat16 [32768, 1152], P(('groups', 'seq')), parts along dimension 0, may hold values from -18 to 18
- vis_proj: bfloat16 [1152, 1792], replicated, may hold values from -0.1875 to 0.1875
- kv_proj: bfloat16 [1792, 512], replicated, may hold values from -0.125 to 0.125
- out_proj: bfloat16 [1792, 1792], P(None, 'seq'), may hold values from -0.125 to 0.125
- queries: bfloat16 [256, 1792], P(('groups', 'seq')), parts along dimension 0, may hold values from -350 to 350
- frame_range: int32 [2, 2], P('groups'), parts along dimension 0, may hold values from 0 to 64, as said below
- text_lens: int32 [2], P('groups'), parts along dimension 0, may hold values from 1 to 128, as said below
Outputs:
- attended: bfloat16 [256, 1792], P(('groups', 'seq')), parts along dimension 0
There are 2 independent parts, one for each index of `groups`. A program takes and returns all parts, laid end to end along the dimension named above; an argument that names none is the same for every part. Nothing has to cross between parts.
Inputs may be any that keep to these rules, and one draw needn't show every extreme that they name: frame_range[b, 0] < frame_range[b, 1] for every block b; some block attends all 64 frames. `text_lens`: some block is full.
All inputs are finite; a program needn't handle non-finite values.
Results may differ from a plain program's by a relative error of at most 0.02.
The roundings to bfloat16 on the way count: a program that leaves them out, or rounds other values in their place, can miss the bound.
Values may be sent and summed in bfloat16 or wider, within the bound.
A program may use at most 128 MiB of HBM per device.

v0:
```python
import jax
import jax.numpy as jnp
from jax import lax
from jax.sharding import PartitionSpec as P

HEADS = 14
KV_HEADS = 2
HEAD_DIM = 128
FRAME_TOK = 256
QBLK = 128
NEG = -1e30


def fresh_state(row_count):
    return (
        jnp.zeros((row_count, HEADS * HEAD_DIM), jnp.float32),
        jnp.full((row_count, HEADS), NEG, jnp.float32),
        jnp.zeros((row_count, HEADS), jnp.float32),
    )


def absorb(running, query_rows, key_rows, value_rows, allowed):
    output_sum, maxima, totals = running
    row_count = query_rows.shape[0]
    group_size = HEADS // KV_HEADS
    query_heads = query_rows.reshape(row_count, KV_HEADS, group_size, HEAD_DIM)
    scores = jnp.einsum(
        "tkgd,rkd->tkgr", query_heads, key_rows, preferred_element_type=jnp.float32
    ) * HEAD_DIM ** (-0.5)
    masked = jnp.where(allowed, scores, NEG)
    new_maxima = jnp.maximum(maxima, jnp.max(masked, axis=-1).reshape(row_count, HEADS))
    shaped = new_maxima.reshape(row_count, KV_HEADS, group_size)
    weights = jnp.where(allowed, jnp.exp(scores - shaped[..., None]), 0.0)
    new_totals = jnp.sum(weights, axis=-1).reshape(row_count, HEADS)
    blended = jnp.einsum(
        "tkgr,rkd->tkgd",
        weights.astype(jnp.bfloat16),
        value_rows,
        preferred_element_type=jnp.float32,
    )
    new_sum = blended.reshape(row_count, HEADS, HEAD_DIM)
    return (new_sum.reshape(row_count, HEADS * HEAD_DIM), new_maxima, new_totals)


def visit_keys(running, query_rows, key_rows, value_rows, frame_range, block_id, first_row):
    local_count = key_rows.shape[0]
    bounds = lax.dynamic_index_in_dim(frame_range, block_id, 0, keepdims=False)
    frames = (first_row + jnp.arange(local_count, dtype=jnp.int32)) // FRAME_TOK
    allowed = (frames >= bounds[0]) & (frames < bounds[1])
    result = absorb(running, query_rows, key_rows, value_rows, allowed)
    return result


def body(visual, vis_proj, kv_proj, out_proj, queries, frame_range, text_lens):
    devices = lax.axis_size("seq")
    my_index = lax.axis_index("seq")
    hidden = jax.nn.gelu(
        jnp.dot(visual, vis_proj, preferred_element_type=jnp.float32), approximate=True
    ).astype(jnp.bfloat16)
    key_value = jnp.dot(hidden, kv_proj, preferred_element_type=jnp.float32).astype(jnp.bfloat16)
    kv_width = KV_HEADS * HEAD_DIM
    local_count = visual.shape[0]
    key_rows = key_value[:, :kv_width].reshape(local_count, KV_HEADS, HEAD_DIM)
    value_rows = key_value[:, kv_width:].reshape(local_count, KV_HEADS, HEAD_DIM)
    first_row = my_index * local_count
    own_count = queries.shape[0]

    def visit_local(running, query_rows, block_id):
        return visit_keys(
            running, query_rows, key_rows, value_rows, frame_range, block_id, first_row
        )

    every_query = lax.all_gather(queries, "seq", axis=0, tiled=True)
    block_count = every_query.shape[0] // QBLK
    stacked = every_query.reshape(block_count, QBLK, HEADS * HEAD_DIM)

    def one_block(packed):
        block_rows, block_id = packed
        return visit_local(fresh_state(QBLK), block_rows, block_id)

    sums_all, maxima_all, totals_all = lax.map(
        one_block, (stacked, jnp.arange(block_count, dtype=jnp.int32))
    )
    part_sums, part_maxima, part_totals = (
        lax.all_to_all(
            sums_all.reshape(1, block_count * QBLK, HEADS * HEAD_DIM),
            "seq",
            split_axis=1,
            concat_axis=0,
            tiled=True,
        ),
        lax.all_to_all(
            maxima_all.reshape(1, block_count * QBLK, HEADS),
            "seq",
            split_axis=1,
            concat_axis=0,
            tiled=True,
        ),
        lax.all_to_all(
            totals_all.reshape(1, block_count * QBLK, HEADS),
            "seq",
            split_axis=1,
            concat_axis=0,
            tiled=True,
        ),
    )
    maxima = jnp.max(part_maxima, axis=0)
    scaling = jnp.exp(part_maxima - maxima[None])
    totals = jnp.sum(scaling * part_totals, axis=0)
    weighted = part_sums.reshape(devices, own_count, HEADS, HEAD_DIM) * scaling[..., None]
    output_sum = jnp.sum(weighted, axis=0).reshape(own_count, HEADS * HEAD_DIM)
    normed = output_sum.reshape(own_count, HEADS, HEAD_DIM) / totals[..., None]
    my_block = my_index * own_count // QBLK
    length = lax.dynamic_index_in_dim(text_lens, my_block, 0, keepdims=False)
    positions = my_index * own_count % QBLK + jnp.arange(own_count, dtype=jnp.int32)
    attention = (
        jnp.where((positions < length)[:, None, None], normed, 0.0)
        .reshape(own_count, HEADS * HEAD_DIM)
        .astype(jnp.bfloat16)
    )
    return jnp.dot(
        attention,
        lax.all_gather(out_proj, "seq", axis=1, tiled=True),
        preferred_element_type=jnp.float32,
    ).astype(jnp.bfloat16)


def solution(mesh):
    placed = (
        P(("groups", "seq"), None),
        P(),
        P(),
        P(None, "seq"),
        P(("groups", "seq"), None),
        P("groups", None),
        P("groups"),
    )
    return jax.shard_map(
        body, mesh=mesh, in_specs=placed, out_specs=P(("groups", "seq"), None), check_vma=False
    )
```

profile of v0, /device:TPU:9, one launch (start us, length us, event | category | flops | bytes accessed | tf_op | source)
XLA Modules:
  0.0 117.4 jit_solution(4725177874971610116)
XLA Ops:
  6.5 0.0 copy-start
  6.5 0.0 all-gather.2.cloned.1.call-start
  6.5 0.7 all-gather.2.cloned.1.call-update
  7.3 22.1 %all_gather.6 = bf16[128,1792]{1,0:T(8,128)(2,1)S(1)} all-gather(bf16[8,1792]{1,0:T(8,128)(2,1)} %param.11), channel_id=1, replica_groups=mesh['groups'=2,'seq'=16] {'seq'}, dimensions={0}, use_global_device_ids=true | all-gather | bytes 487424 | tf_op jit(solution)/shard_map/all_gather | solution.py:73
  29.4 0.3 copy.16
  29.7 1.3 %fusion.39 = (s32[1,1]{1,0:T(1,128)}, s32[1,1]{1,0:T(1,128)}) fusion(s32[1,2]{1,0:T(1,128)} %param.12), kind=kLoop, calls=%fused_computation.51 | loop fusion | bytes 16 | tf_op jit(solution)/shard_map/while/body/eval_jaxpr/slice | solution.py:49
  31.0 1.2 %compare_and_fusion = pred[1024]{0:T(1024)(128)(4,1)S(1)} fusion(s32[]{:T(128)} %bitcast.5, s32[]{:T(128)} %bitcast.4, s32[]{:T(128)S(6)} %mul.69), kind=kLoop, calls=%fused_computation.41 | loop fusion | flops 19456 | bytes 1036 | tf_op jit(solution)/shard_map/while/body/eval_jaxpr/and | solution.py:49
  32.2 0.0 copy-done
  32.2 11.2 %fusion.18 = bf16[1024,512]{0,1:T(8,128)(2,1)} fusion(bf16[1792,512]{1,0:T(8,128)(2,1)} %param.9, bf16[1024,1152]{1,0:T(8,128)(2,1)S(1)} %copy-done, bf16[1152,1792]{1,0:T(8,128)(2,1)} %param.8), kind=kOutput, calls=%fused_computation.20 | convolution fusion | flops 6123945984 | bytes 9371648 | tf_op jit(solution)/shard_map/dot_general | solution.py:60
  43.4 2.1 %fusion.38 = (bf16[1024,256]{0,1:T(8,128)(2,1)S(1)}, bf16[1024,256]{0,1:T(8,128)(2,1)}) fusion(bf16[1024,512]{0,1:T(8,128)(2,1)} %fusion.18), kind=kLoop, calls=%fused_computation.50 | loop fusion | bytes 2097152 | tf_op jit(solution)/shard_map/slice | solution.py:63
  45.5 1.6 %fusion.8 = (f32[128,2,7]{0,2,1:T(8,128)S(1)}, f32[2,1024,128,7]{2,1,3,0:T(8,128)S(1)}) fusion(pred[1024]{0:T(1024)(128)(4,1)S(1)} %compare_and_fusion, bf16[1024,2,128,1]{0,2,3,1:T(8,128)(2,1)S(1)} %bitcast.58, bf16[128,2,7,128]{0,3,2,1:T(8,128)(2,1)S(1)} %bitcast.59), kind=kOutput, calls=%fused_computation.11 | convolution fusion | flops 475265280 | bytes 8331264 | tf_op jit(solution)/shard_map/while/body/eval_jaxpr/tkgd,rkd->tkgr/dot_general | solution.py:27
  47.1 0.0 copy-start.1
  47.1 2.9 %copy-done.1 = f32[2,1024,128,7]{2,1,3,0:T(8,128)} copy-done((f32[2,1024,128,7]{2,1,3,0:T(8,128)}, f32[2,1024,128,7]{2,1,3,0:T(8,128)S(1)}, u32[]{:S(2)}) %copy-start.1) | copy-done | bytes 7340056
  50.1 2.0 %fusion.11 = f32[128,2,7]{0,2,1:T(8,128)S(1)} fusion(f32[2,1024,128,7]{2,1,3,0:T(8,128)S(1)} %get-tuple-element.38, f32[128,2,7]{0,2,1:T(8,128)S(1)} %broadcast_maximum_fusion, pred[1024]{0:T(1024)(128)(4,1)S(1)} %compare_and_fusion), kind=kLoop, calls=%fused_computation.14 | loop fusion | flops 7338240 | bytes 7355392 | tf_op jit(solution)/shard_map/while/body/eval_jaxpr/reduce_sum | solution.py:34
  52.0 0.7 copy.24
  52.8 6.3 %all-to-all-start.2 = ((f32[1,128,14]{2,0,1:T(1,128)}), f32[1,128,14]{2,0,1:T(1,128)S(1)}, u32[]{:S(2)}, u32[]{:S(2)}) async-start(f32[1,128,14]{2,0,1:T(1,128)} %copy.24), calls=%async_computation.2 | async-start | bytes 131072 | tf_op jit(solution)/shard_map/all_to_all | solution.py:99
  59.1 0.7 copy.21
  59.8 4.5 %all-to-all-done.2 = f32[1,128,14]{2,0,1:T(1,128)S(1)} async-done(((f32[1,128,14]{2,0,1:T(1,128)}), f32[1,128,14]{2,0,1:T(1,128)S(1)}, u32[]{:S(2)}, u32[]{:S(2)}) %all-to-all-start.2) | async-done | bytes 7200 | tf_op jit(solution)/shard_map/all_to_all | solution.py:99
  64.3 5.4 %all-to-all-start.1 = ((f32[1,128,14]{2,0,1:T(1,128)}), f32[1,128,14]{2,0,1:T(1,128)S(1)}, u32[]{:S(2)}, u32[]{:S(2)}) async-start(f32[1,128,14]{2,0,1:T(1,128)} %copy.21), calls=%async_computation.1 | async-start | bytes 131072 | tf_op jit(solution)/shard_map/all_to_all | solution.py:92
  69.7 4.8 %fusion.13 = f32[2,128,128,7]{2,1,3,0:T(8,128)S(1)} fusion(bf16[1024,2,128,1]{0,2,3,1:T(8,128)(2,1)} %bitcast.63, f32[2,1024,128,7]{2,1,3,0:T(8,128)} %copy-done.1, f32[128,2,7]{0,2,1:T(8,128)S(1)} %broadcast_maximum_fusion, pred[1024]{0:T(1024)(128)(4,1)S(1)} %compare_and_fusion), kind=kOutput, calls=%fused_computation.16 | convolution fusion | flops 477102080 | bytes 8790016 | tf_op jit(solution)/shard_map/while/body/eval_jaxpr/tkgr,rkd->tkgd/dot_general | solution.py:35
  74.5 2.1 %copy.20 = f32[1,128,1792]{2,0,1:T(1,128)} copy(f32[1,128,1792]{1,2,0:T(8,128)S(1)} %bitcast.60) | data formatting | bytes 1835008 | tf_op jit(solution)/shard_map/while/body/jit(dynamic_update_index_in_dim)/broadcast_in_dim | solution.py:81
  76.6 0.0 all-to-all-done.1
  76.6 6.2 %all-to-all-start = ((f32[1,128,1792]{2,0,1:T(1,128)}), f32[1,128,1792]{2,0,1:T(1,128)S(1)}, u32[]{:S(2)}, u32[]{:S(2)}) async-start(f32[1,128,1792]{2,0,1:T(1,128)} %copy.20), calls=%async_computation | async-start | bytes 1835008 | tf_op jit(solution)/shard_map/all_to_all | solution.py:85
  83.4 0.2 copy.33
  83.6 0.8 copy.32
  84.5 0.1 copy.35
  84.6 0.9 multiply_reduce_fusion
  85.6 19.4 %all-to-all-done = f32[1,128,1792]{2,0,1:T(1,128)S(1)} async-done(((f32[1,128,1792]{2,0,1:T(1,128)}), f32[1,128,1792]{2,0,1:T(1,128)S(1)}, u32[]{:S(2)}, u32[]{:S(2)}) %all-to-all-start) | async-done | bytes 917536 | tf_op jit(solution)/shard_map/all_to_all | solution.py:85
  105.0 0.3 fusion.21
  105.3 0.0 all-gather.2.cloned.1.call-done
  105.3 5.2 %convolution_convert_fusion = bf16[8,1792]{1,0:T(8,128)(2,1)} fusion(bf16[1792,1792]{0,1:T(8,128)(2,1)} %all-gather.2.cloned.1.call-done, f32[8,1792]{1,0:T(8,128)S(1)} %fusion.21, f32[8,14]{0,1:T(8,128)S(1)} %get-tuple-element.21, pred[8]{0:T(512)(128)(4,1)S(1)} %add_compare_fusion), kind=kOutput, calls=%fused_computation.19 | convolution fusion | flops 51437568 | bytes 6509000 | tf_op jit(solution)/shard_map/dot_general | solution.py:121
  (6 shorter events, 0.1 us)
Async XLA Ops:
  6.5 25.7 %copy-start = (bf16[1024,1152]{1,0:T(8,128)(2,1)S(1)}, bf16[1024,1152]{1,0:T(8,128)(2,1)}, u32[]{:S(2)}) copy-start(bf16[1024,1152]{1,0:T(8,128)(2,1)} %param.7) | copy-start | bytes 7077892
  6.5 98.8 %all-gather.2.cloned.1.call-start = ((), (), s32[]{:S(2)}) async-start(), calls=%async_computation.3 | async-start | bytes 6823936 | tf_op jit(solution)/shard_map/all_gather | solution.py:123
  47.1 3.0 %copy-start.1 = (f32[2,1024,128,7]{2,1,3,0:T(8,128)}, f32[2,1024,128,7]{2,1,3,0:T(8,128)S(1)}, u32[]{:S(2)}) copy-start(f32[2,1024,128,7]{2,1,3,0:T(8,128)S(1)} %get-tuple-element.38) | copy-start | bytes 22020100
  52.8 11.5 %all-to-all-start.2 = ((f32[1,128,14]{2,0,1:T(1,128)}), f32[1,128,14]{2,0,1:T(1,128)S(1)}, u32[]{:S(2)}, u32[]{:S(2)}) async-start(f32[1,128,14]{2,0,1:T(1,128)} %copy.24), calls=%async_computation.2 | async-start | bytes 131072 | tf_op jit(solution)/shard_map/all_to_all | solution.py:99
  64.3 12.3 %all-to-all-start.1 = ((f32[1,128,14]{2,0,1:T(1,128)}), f32[1,128,14]{2,0,1:T(1,128)S(1)}, u32[]{:S(2)}, u32[]{:S(2)}) async-start(f32[1,128,14]{2,0,1:T(1,128)} %copy.21), calls=%async_computation.1 | async-start | bytes 131072 | tf_op jit(solution)/shard_map/all_to_all | solution.py:92
  76.6 28.4 %all-to-all-start = ((f32[1,128,1792]{2,0,1:T(1,128)}), f32[1,128,1792]{2,0,1:T(1,128)S(1)}, u32[]{:S(2)}, u32[]{:S(2)}) async-start(f32[1,128,1792]{2,0,1:T(1,128)} %copy.20), calls=%async_computation | async-start | bytes 1835008 | tf_op jit(solution)/shard_map/all_to_all | solution.py:85
Sparse Core Ops, SparseCore 0:
  9.6 64.7 all-gather.1
where the time goes:
time: 118 us; the launch traced here: 117 us
  waiting for transfers between devices  24.6 us (21%)
  matrix products  22.8 us (19%)
  blocking collectives  22.1 us (19%)
  starting transfers between devices  17.9 us (15%)
  between operations  14.1 us (12%)
  local copies, waits for them, and re-layouts  11.3 us (10%)
  other arithmetic  4.46 us (4%)
    all_gather x1, blocking collectives, body(): every_query = lax.all_gather(queries, 'seq', axis=0, tiled=True)  22.1 us
    all_to_all x1, waiting for transfers between devices, body(): lax.all_to_all(sums_all.reshape(1, block_count * QBLK, HEADS * HEAD_DIM),...  19.4 us
    dot_general x1, matrix products, body(): jnp.dot(hidden, kv_proj, preferred_element_type=jnp.float32)  11.2 us
    all_to_all x1, starting transfers between devices, body(): lax.all_to_all(totals_all.reshape(1, block_count * QBLK, HEADS), 'seq', s...  6.29 us
    all_to_all x1, starting transfers between devices, body(): lax.all_to_all(sums_all.reshape(1, block_count * QBLK, HEADS * HEAD_DIM),...  6.16 us
    all_to_all x1, starting transfers between devices, body(): lax.all_to_all(maxima_all.reshape(1, block_count * QBLK, HEADS), 'seq', s...  5.45 us
    dot_general x1, matrix products, body(): jnp.dot(attention, lax.all_gather(out_proj, 'seq', axis=1, tiled=True), p...  5.24 us
    dot_general x1, matrix products, absorb(): jnp.einsum('tkgr,rkd->tkgd', weights.astype(jnp.bfloat16), value_rows, pr...  4.78 us
  transfers between devices with their start and end apart: 4, of which 2 were waited for; matrix products, arithmetic and copies ran while one was open for 26% of the time, Pallas kernels for 0%

commit v1 on v0

--- a/solution.py
+++ b/solution.py
@@ -70,7 +70,21 @@
             running, query_rows, key_rows, value_rows, frame_range, block_id, first_row
         )
 
-    every_query = lax.all_gather(queries, "seq", axis=0, tiled=True)
+    ways, here, turn = (lax.axis_size("seq"), lax.axis_index("seq"), queries.shape[0])
+    shape = [n * ways if d == 0 else n for d, n in enumerate(queries.shape)]
+    full = lax.dynamic_update_slice_in_dim(
+        jnp.zeros(shape, queries.dtype), queries, here * turn, axis=0
+    )
+    going_up = going_down = queries
+    for far in range(1, ways // 2 + 1):
+        going_up = lax.ppermute(going_up, "seq", [(d, (d + 1) % ways) for d in range(ways)])
+        full = lax.dynamic_update_slice_in_dim(full, going_up, (here - far) % ways * turn, axis=0)
+        if 2 * far < ways:
+            going_down = lax.ppermute(going_down, "seq", [(d, (d - 1) % ways) for d in range(ways)])
+            full = lax.dynamic_update_slice_in_dim(
+                full, going_down, (here + far) % ways * turn, axis=0
+            )
+    every_query = full
     block_count = every_query.shape[0] // QBLK
     stacked = every_query.reshape(block_count, QBLK, HEADS * HEAD_DIM)
 

time: 118 us -> 285 us (2.42)
  local copies, waits for them, and re-layouts: 11.3 us -> 106 us
  waiting for transfers between devices: 24.6 us -> 87.6 us
  starting transfers between devices: 17.9 us -> 45.1 us
  blocking collectives: 22.1 us -> 0 us
    dynamic_update_slice x0 -> x16, local copies, waits for them, and re-layouts: none -> 94.1 us  [the longest x8 46.8 us: body(): lax.dynamic_update_slice_in_dim(full, going_up, (here - far) % ways * tur...]
    ppermute x0 -> x15, waiting for transfers between devices: none -> 63.1 us  [the longest x8 34.9 us: body(): lax.ppermute(going_up, 'seq', [(d, (d + 1) % ways) for d in range(ways)])]
    all_gather x1 -> x0, blocking collectives: 22.1 us -> none  [body(): every_query = lax.all_gather(queries, 'seq', axis=0, tiled=True)]
    ppermute x0 -> x15, starting transfers between devices: none -> 20.7 us  [the longest x8 19 us: body(): lax.ppermute(going_up, 'seq', [(d, (d + 1) % ways) for d in range(ways)])]
    all_to_all x1, starting transfers between devices: 6.29 us -> 13.1 us  [body(): lax.all_to_all(totals_all.reshape(1, block_count * QBLK, HEADS), 'seq', s...]
  transfers between devices with their start and end apart: 4 -> 19, of which waited for: 2 -> 13; matrix products, arithmetic and copies ran while one was open for 26% -> 45% of each run, Pallas kernels for 0% -> 0%
where the time goes in v1:
time: 285 us; the launch traced here: 282 us
  local copies, waits for them, and re-layouts  106 us (37%)
  waiting for transfers between devices  87.6 us (31%)
  starting transfers between devices  45.1 us (16%)
  matrix products  23.8 us (8%)
  between operations  14.5 us (5%)
  other arithmetic  4.51 us (2%)
    dynamic_update_slice x8, local copies, waits for them, and re-layouts, body(): lax.dynamic_update_slice_in_dim(full, going_up, (here - far) % ways * tur...  46.8 us
    dynamic_update_slice x7, local copies, waits for them, and re-layouts, body(): lax.dynamic_update_slice_in_dim(full, going_down, (here + far) % ways * t...  41.6 us
    ppermute x8, waiting for transfers between devices, body(): lax.ppermute(going_up, 'seq', [(d, (d + 1) % ways) for d in range(ways)])  34.9 us
    ppermute x7, waiting for transfers between devices, body(): lax.ppermute(going_down, 'seq', [(d, (d - 1) % ways) for d in range(ways)])  28.1 us
    all_to_all x1, waiting for transfers between devices, body(): lax.all_to_all(sums_all.reshape(1, block_count * QBLK, HEADS * HEAD_DIM),...  19.4 us
    ppermute x8, starting transfers between devices, body(): lax.ppermute(going_up, 'seq', [(d, (d + 1) % ways) for d in range(ways)])  19 us
    all_to_all x1, starting transfers between devices, body(): lax.all_to_all(totals_all.reshape(1, block_count * QBLK, HEADS), 'seq', s...  13.1 us
    dot_general x1, matrix products, body(): jnp.dot(hidden, kv_proj, preferred_element_type=jnp.float32)  11.2 us
  transfers between devices with their start and end apart: 19, of which 13 were waited for; matrix products, arithmetic and copies ran while one was open for 45% of the time, Pallas kernels for 0%

profile of v1, /device:TPU:9, one launch (start us, length us, event | category | flops | bytes accessed | tf_op | source)
XLA Modules:
  0.0 281.7 jit_solution(3832703095600176747)
XLA Ops:
  10.2 11.4 %collective-permute-done = bf16[8,1792]{0,1:T(8,128)(2,1)S(1)} collective-permute-done((bf16[8,1792]{0,1:T(8,128)(2,1)S(1)}, bf16[8,1792]{0,1:T(8,128)(2,1)S(1)}, u32[]{:S(2)}, u32[]{:S(2)}) %collective-permute-start) | collective-permute-done | bytes 28704 | tf_op jit(solution)/shard_map/ppermute | solution.py:80
  25.7 6.6 %collective-permute-done.2 = bf16[8,1792]{0,1:T(8,128)(2,1)S(1)} collective-permute-done((bf16[8,1792]{0,1:T(8,128)(2,1)S(1)}, bf16[8,1792]{0,1:T(8,128)(2,1)S(1)}, u32[]{:S(2)}, u32[]{:S(2)}) %collective-permute-start.2) | collective-permute-done | bytes 28704 | tf_op jit(solution)/shard_map/ppermute | solution.py:80
  38.4 3.5 %collective-permute-done.4 = bf16[8,1792]{0,1:T(8,128)(2,1)S(1)} collective-permute-done((bf16[8,1792]{0,1:T(8,128)(2,1)S(1)}, bf16[8,1792]{0,1:T(8,128)(2,1)S(1)}, u32[]{:S(2)}, u32[]{:S(2)}) %collective-permute-start.4) | collective-permute-done | bytes 28704 | tf_op jit(solution)/shard_map/ppermute | solution.py:80
  44.3 9.2 %collective-permute-done.5 = bf16[8,1792]{0,1:T(8,128)(2,1)} collective-permute-done((bf16[8,1792]{0,1:T(8,128)(2,1)S(1)}, bf16[8,1792]{0,1:T(8,128)(2,1)}, u32[]{:S(2)}, u32[]{:S(2)}) %collective-permute-start.5) | collective-permute-done | bytes 28704 | tf_op jit(solution)/shard_map/ppermute | solution.py:83
  53.6 11.7 %collective-permute-done.6 = bf16[8,1792]{0,1:T(8,128)(2,1)} collective-permute-done((bf16[8,1792]{0,1:T(8,128)(2,1)S(1)}, bf16[8,1792]{0,1:T(8,128)(2,1)}, u32[]{:S(2)}, u32[]{:S(2)}) %collective-permute-start.6) | collective-permute-done | bytes 28704 | tf_op jit(solution)/shard_map/ppermute | solution.py:80
  65.2 2.9 %collective-permute-start.8 = (bf16[8,1792]{0,1:T(8,128)(2,1)}, bf16[8,1792]{0,1:T(8,128)(2,1)}, u32[]{:S(2)}, u32[]{:S(2)}) collective-permute-start(bf16[8,1792]{0,1:T(8,128)(2,1)} %collective-permute-done.6), channel_id=1, source_target_pairs={{0,1},{1,2},{2,3},{3,4},{4,5},{5,6},{6,7},{7,8},{8,9},{9,10},{10,1... | collective-permute-start | bytes 86024 | tf_op jit(solution)/shard_map/ppermute | solution.py:80
  68.2 11.2 %fusion.18 = bf16[1024,512]{0,1:T(8,128)(2,1)} fusion(bf16[1792,512]{1,0:T(8,128)(2,1)} %param.9, bf16[1024,1152]{1,0:T(8,128)(2,1)S(1)} %copy-done, bf16[1152,1792]{1,0:T(8,128)(2,1)} %param.8), kind=kOutput, calls=%fused_computation.20 | convolution fusion | flops 6123945984 | bytes 9371648 | tf_op jit(solution)/shard_map/dot_general | solution.py:60
  85.5 4.8 %collective-permute-done.9 = bf16[8,1792]{0,1:T(8,128)(2,1)} collective-permute-done((bf16[8,1792]{0,1:T(8,128)(2,1)}, bf16[8,1792]{0,1:T(8,128)(2,1)}, u32[]{:S(2)}, u32[]{:S(2)}) %collective-permute-start.9) | collective-permute-done | bytes 28704 | tf_op jit(solution)/shard_map/ppermute | solution.py:83
  93.7 10.6 %collective-permute-done.11 = bf16[8,1792]{0,1:T(8,128)(2,1)} collective-permute-done((bf16[8,1792]{0,1:T(8,128)(2,1)}, bf16[8,1792]{0,1:T(8,128)(2,1)}, u32[]{:S(2)}, u32[]{:S(2)}) %collective-permute-start.11) | collective-permute-done | bytes 28704 | tf_op jit(solution)/shard_map/ppermute | solution.py:83
  108.4 5.7 %dynamic_update_slice.88 = bf16[128,1792]{0,1:T(8,128)(2,1)} dynamic-update-slice(bf16[128,1792]{0,1:T(8,128)(2,1)} %squeeze.26, bf16[8,1792]{0,1:T(8,128)(2,1)S(1)} %copy.18, s32[]{:T(128)S(6)} %select_n.144, s32[]{:T(128)} %constant.188.clone.1) | dynamic-update-slice | bytes 57348 | tf_op jit(solution)/shard_map/dynamic_update_slice | solution.py:75
  114.1 5.9 %dynamic_update_slice.89 = bf16[128,1792]{0,1:T(8,128)(2,1)} dynamic-update-slice(bf16[128,1792]{0,1:T(8,128)(2,1)} %dynamic_update_slice.88, bf16[8,1792]{0,1:T(8,128)(2,1)} %copy-done.2, s32[]{:T(128)S(6)} %select_n.146, s32[]{:T(128)} %constant.188.clone.1) | dynamic-update-slice | bytes 57348 | tf_op jit(solution)/shard_map/dynamic_update_slice | solution.py:81
  120.1 5.9 %dynamic_update_slice.90 = bf16[128,1792]{0,1:T(8,128)(2,1)} dynamic-update-slice(bf16[128,1792]{0,1:T(8,128)(2,1)} %dynamic_update_slice.89, bf16[8,1792]{0,1:T(8,128)(2,1)} %copy-done.3, s32[]{:T(128)S(6)} %select_n.148, s32[]{:T(128)} %constant.188.clone.1) | dynamic-update-slice | bytes 57348 | tf_op jit(solution)/shard_map/dynamic_update_slice | solution.py:84
  126.0 5.9 %dynamic_update_slice.91 = bf16[128,1792]{0,1:T(8,128)(2,1)} dynamic-update-slice(bf16[128,1792]{0,1:T(8,128)(2,1)} %dynamic_update_slice.90, bf16[8,1792]{0,1:T(8,128)(2,1)} %copy-done.4, s32[]{:T(128)S(6)} %select_n.150, s32[]{:T(128)} %constant.188.clone.1) | dynamic-update-slice | bytes 57348 | tf_op jit(solution)/shard_map/dynamic_update_slice | solution.py:81
  132.0 5.9 %dynamic_update_slice.92 = bf16[128,1792]{0,1:T(8,128)(2,1)} dynamic-update-slice(bf16[128,1792]{0,1:T(8,128)(2,1)} %dynamic_update_slice.91, bf16[8,1792]{0,1:T(8,128)(2,1)} %copy-done.5, s32[]{:T(128)S(6)} %select_n.152, s32[]{:T(128)} %constant.188.clone.1) | dynamic-update-slice | bytes 57348 | tf_op jit(solution)/shard_map/dynamic_update_slice | solution.py:84
  137.9 5.9 %dynamic_update_slice.93 = bf16[128,1792]{0,1:T(8,128)(2,1)} dynamic-update-slice(bf16[128,1792]{0,1:T(8,128)(2,1)} %dynamic_update_slice.92, bf16[8,1792]{0,1:T(8,128)(2,1)} %copy-done.6, s32[]{:T(128)S(6)} %select_n.154, s32[]{:T(128)} %constant.188.clone.1) | dynamic-update-slice | bytes 57348 | tf_op jit(solution)/shard_map/dynamic_update_slice | solution.py:81
  143.9 5.9 %dynamic_update_slice.94 = bf16[128,1792]{0,1:T(8,128)(2,1)} dynamic-update-slice(bf16[128,1792]{0,1:T(8,128)(2,1)} %dynamic_update_slice.93, bf16[8,1792]{0,1:T(8,128)(2,1)} %collective-permute-done.5, s32[]{:T(128)S(6)} %select_n.156, s32[]{:T(128)} %constant.188.clone.1) | dynamic-update-slice | bytes 57348 | tf_op jit(solution)/shard_map/dynamic_update_slice | solution.py:84
  149.8 5.9 %dynamic_update_slice.95 = bf16[128,1792]{0,1:T(8,128)(2,1)} dynamic-update-slice(bf16[128,1792]{0,1:T(8,128)(2,1)} %dynamic_update_slice.94, bf16[8,1792]{0,1:T(8,128)(2,1)} %collective-permute-done.6, s32[]{:T(128)S(6)} %select_n.158, s32[]{:T(128)} %constant.188.clone.1) | dynamic-update-slice | bytes 57348 | tf_op jit(solution)/shard_map/dynamic_update_slice | solution.py:81
  155.8 5.9 %dynamic_update_slice.96 = bf16[128,1792]{0,1:T(8,128)(2,1)} dynamic-update-slice(bf16[128,1792]{0,1:T(8,128)(2,1)} %dynamic_update_slice.95, bf16[8,1792]{0,1:T(8,128)(2,1)} %collective-permute-done.7, s32[]{:T(128)S(6)} %select_n.160, s32[]{:T(128)} %constant.188.clone.1) | dynamic-update-slice | bytes 57348 | tf_op jit(solution)/shard_map/dynamic_update_slice | solution.py:84
  161.7 5.1 %dynamic_update_slice.97 = bf16[128,1792]{0,1:T(8,128)(2,1)} dynamic-update-slice(bf16[128,1792]{0,1:T(8,128)(2,1)} %dynamic_update_slice.96, bf16[8,1792]{0,1:T(8,128)(2,1)} %collective-permute-done.8, s32[]{:T(128)S(6)} %select_n.162, s32[]{:T(128)} %constant.188.clone.1) | dynamic-update-slice | bytes 57348 | tf_op jit(solution)/shard_map/dynamic_update_slice | solution.py:81
  166.8 5.9 %dynamic_update_slice.98 = bf16[128,1792]{0,1:T(8,128)(2,1)} dynamic-update-slice(bf16[128,1792]{0,1:T(8,128)(2,1)} %dynamic_update_slice.97, bf16[8,1792]{0,1:T(8,128)(2,1)} %collective-permute-done.9, s32[]{:T(128)S(6)} %select_n.164, s32[]{:T(128)} %constant.188.clone.1) | dynamic-update-slice | bytes 57348 | tf_op jit(solution)/shard_map/dynamic_update_slice | solution.py:84
  172.8 5.9 %dynamic_update_slice.99 = bf16[128,1792]{0,1:T(8,128)(2,1)} dynamic-update-slice(bf16[128,1792]{0,1:T(8,128)(2,1)} %dynamic_update_slice.98, bf16[8,1792]{0,1:T(8,128)(2,1)} %collective-permute-done.10, s32[]{:T(128)S(6)} %select_n.166, s32[]{:T(128)} %constant.188.clone.1) | dynamic-update-slice | bytes 57348 | tf_op jit(solution)/shard_map/dynamic_update_slice | solution.py:81
  178.7 5.9 %dynamic_update_slice.100 = bf16[128,1792]{0,1:T(8,128)(2,1)} dynamic-update-slice(bf16[128,1792]{0,1:T(8,128)(2,1)} %dynamic_update_slice.99, bf16[8,1792]{0,1:T(8,128)(2,1)} %collective-permute-done.11, s32[]{:T(128)S(6)} %select_n.168, s32[]{:T(128)} %constant.188.clone.1) | dynamic-update-slice | bytes 57348 | tf_op jit(solution)/shard_map/dynamic_update_slice | solution.py:84
  184.7 5.9 %dynamic_update_slice.101 = bf16[128,1792]{0,1:T(8,128)(2,1)} dynamic-update-slice(bf16[128,1792]{0,1:T(8,128)(2,1)} %dynamic_update_slice.100, bf16[8,1792]{0,1:T(8,128)(2,1)} %collective-permute-done.12, s32[]{:T(128)S(6)} %select_n.170, s32[]{:T(128)} %constant.188.clone.1) | dynamic-update-slice | bytes 57348 | tf_op jit(solution)/shard_map/dynamic_update_slice | solution.py:81
  190.6 6.0 %dynamic_update_slice.102 = bf16[128,1792]{0,1:T(8,128)(2,1)} dynamic-update-slice(bf16[128,1792]{0,1:T(8,128)(2,1)} %dynamic_update_slice.101, bf16[8,1792]{0,1:T(8,128)(2,1)} %collective-permute-done.13, s32[]{:T(128)S(6)} %select_n.172, s32[]{:T(128)} %constant.188.clone.1) | dynamic-update-slice | bytes 57348 | tf_op jit(solution)/shard_map/dynamic_update_slice | solution.py:84
  196.6 6.0 %dynamic_update_slice.103 = bf16[128,1792]{0,1:T(8,128)(2,1)} dynamic-update-slice(bf16[128,1792]{0,1:T(8,128)(2,1)} %dynamic_update_slice.102, bf16[8,1792]{0,1:T(8,128)(2,1)} %collective-permute-done.14, s32[]{:T(128)S(6)} %select_n.174, s32[]{:T(128)} %constant.188.clone.1) | dynamic-update-slice | bytes 57348 | tf_op jit(solution)/shard_map/dynamic_update_slice | solution.py:81
  210.9 13.1 %all-to-all-start.2 = ((f32[1,128,14]{2,0,1:T(1,128)}), f32[1,128,14]{2,0,1:T(1,128)S(1)}, u32[]{:S(2)}, u32[]{:S(2)}) async-start(f32[1,128,14]{2,0,1:T(1,128)} %copy.28), calls=%async_computation.2 | async-start | bytes 131072 | tf_op jit(solution)/shard_map/all_to_all | solution.py:113
  224.7 4.3 %all-to-all-done.2 = f32[1,128,14]{2,0,1:T(1,128)S(1)} async-done(((f32[1,128,14]{2,0,1:T(1,128)}), f32[1,128,14]{2,0,1:T(1,128)S(1)}, u32[]{:S(2)}, u32[]{:S(2)}) %all-to-all-start.2) | async-done | bytes 7200 | tf_op jit(solution)/shard_map/all_to_all | solution.py:113
  229.0 5.2 %all-to-all-start.1 = ((f32[1,128,14]{2,0,1:T(1,128)}), f32[1,128,14]{2,0,1:T(1,128)S(1)}, u32[]{:S(2)}, u32[]{:S(2)}) async-start(f32[1,128,14]{2,0,1:T(1,128)} %copy.25), calls=%async_computation.1 | async-start | bytes 131072 | tf_op jit(solution)/shard_map/all_to_all | solution.py:106
  234.3 4.7 %fusion.13 = f32[2,128,128,7]{2,1,3,0:T(8,128)S(1)} fusion(bf16[1024,2,128,1]{0,2,3,1:T(8,128)(2,1)} %bitcast.63, f32[2,1024,128,7]{2,1,3,0:T(8,128)} %copy-done.1, f32[128,2,7]{0,2,1:T(8,128)S(1)} %broadcast_maximum_fusion, pred[1024]{0:T(1024)(128)(4,1)S(1)} %compare_and_fusion), kind=kOutput, calls=%fused_computation.16 | convolution fusion | flops 477102080 | bytes 8790016 | tf_op jit(solution)/shard_map/while/body/eval_jaxpr/tkgr,rkd->tkgd/dot_general | solution.py:35
  241.0 6.1 %all-to-all-start = ((f32[1,128,1792]{2,0,1:T(1,128)}), f32[1,128,1792]{2,0,1:T(1,128)S(1)}, u32[]{:S(2)}, u32[]{:S(2)}) async-start(f32[1,128,1792]{2,0,1:T(1,128)} %copy.24), calls=%async_computation | async-start | bytes 1835008 | tf_op jit(solution)/shard_map/all_to_all | solution.py:99
  249.9 19.4 %all-to-all-done = f32[1,128,1792]{2,0,1:T(1,128)S(1)} async-done(((f32[1,128,1792]{2,0,1:T(1,128)}), f32[1,128,1792]{2,0,1:T(1,128)S(1)}, u32[]{:S(2)}, u32[]{:S(2)}) %all-to-all-start) | async-done | bytes 917536 | tf_op jit(solution)/shard_map/all_to_all | solution.py:99
  269.6 5.2 %convolution_convert_fusion = bf16[8,1792]{1,0:T(8,128)(2,1)} fusion(bf16[1792,1792]{0,1:T(8,128)(2,1)} %all-gather.2.cloned.1.call-done, f32[8,1792]{1,0:T(8,128)S(1)} %fusion.21, f32[8,14]{0,1:T(8,128)S(1)} %get-tuple-element.21, pred[8]{0:T(512)(128)(4,1)S(1)} %add_compare_fusion), kind=kOutput, calls=%fused_computation.19 | convolution fusion | flops 51437568 | bytes 6509000 | tf_op jit(solution)/shard_map/dot_general | solution.py:135
  (63 shorter events, 43.1 us)
Async XLA Ops:
  6.5 61.6 %copy-start = (bf16[1024,1152]{1,0:T(8,128)(2,1)S(1)}, bf16[1024,1152]{1,0:T(8,128)(2,1)}, u32[]{:S(2)}) copy-start(bf16[1024,1152]{1,0:T(8,128)(2,1)} %param.7) | copy-start | bytes 7077892
  6.5 263.1 %all-gather.2.cloned.1.call-start = ((), (), s32[]{:S(2)}) async-start(), calls=%async_computation.3 | async-start | bytes 6823936 | tf_op jit(solution)/shard_map/all_gather | solution.py:137
  8.3 84.7 %copy-start.7 = (s32[1,2]{1,0:T(1,128)S(1)}, s32[1,2]{1,0:T(1,128)}, u32[]{:S(2)}) copy-start(s32[1,2]{1,0:T(1,128)} %param.12) | copy-start | bytes 28
  8.3 13.3 %collective-permute-start = (bf16[8,1792]{0,1:T(8,128)(2,1)S(1)}, bf16[8,1792]{0,1:T(8,128)(2,1)S(1)}, u32[]{:S(2)}, u32[]{:S(2)}) collective-permute-start(bf16[8,1792]{0,1:T(8,128)(2,1)S(1)} %copy.18), channel_id=1, source_target_pairs={{0,1},{1,2},{2,3},{3,4},{4,5},{5,6},{6,7},{7,8},{8,9},{9,10},{10,1... | collective-permute-start | bytes 86024 | tf_op jit(solution)/shard_map/ppermute | solution.py:80
  10.2 15.6 %collective-permute-start.1 = (bf16[8,1792]{0,1:T(8,128)(2,1)S(1)}, bf16[8,1792]{0,1:T(8,128)(2,1)S(1)}, u32[]{:S(2)}, u32[]{:S(2)}) collective-permute-start(bf16[8,1792]{0,1:T(8,128)(2,1)S(1)} %copy.18), channel_id=1, source_target_pairs={{0,15},{1,0},{2,1},{3,2},{4,3},{5,4},{6,5},{7,6},{8,7},{9,8},{10,9... | collective-permute-start | bytes 86024 | tf_op jit(solution)/shard_map/ppermute | solution.py:83
  21.6 57.8 %copy-start.2 = (bf16[8,1792]{0,1:T(8,128)(2,1)}, bf16[8,1792]{0,1:T(8,128)(2,1)S(1)}, u32[]{:S(2)}) copy-start(bf16[8,1792]{0,1:T(8,128)(2,1)S(1)} %collective-permute-done) | copy-start | bytes 86020
  21.6 10.7 %collective-permute-start.2 = (bf16[8,1792]{0,1:T(8,128)(2,1)S(1)}, bf16[8,1792]{0,1:T(8,128)(2,1)S(1)}, u32[]{:S(2)}, u32[]{:S(2)}) collective-permute-start(bf16[8,1792]{0,1:T(8,128)(2,1)S(1)} %collective-permute-done), channel_id=1, source_target_pairs={{0,1},{1,2},{2,3},{3,4},{4,5},{5,6},{6,7},{7,8},{8,9},{9,10},{10,1... | collective-permute-start | bytes 86024 | tf_op jit(solution)/shard_map/ppermute | solution.py:80
  25.7 6.6 %copy-start.3 = (bf16[8,1792]{0,1:T(8,128)(2,1)}, bf16[8,1792]{0,1:T(8,128)(2,1)S(1)}, u32[]{:S(2)}) copy-start(bf16[8,1792]{0,1:T(8,128)(2,1)S(1)} %collective-permute-done.1) | copy-start | bytes 86020
  25.7 10.9 %collective-permute-start.3 = (bf16[8,1792]{0,1:T(8,128)(2,1)S(1)}, bf16[8,1792]{0,1:T(8,128)(2,1)S(1)}, u32[]{:S(2)}, u32[]{:S(2)}) collective-permute-start(bf16[8,1792]{0,1:T(8,128)(2,1)S(1)} %collective-permute-done.1), channel_id=1, source_target_pairs={{0,15},{1,0},{2,1},{3,2},{4,3},{5,4},{6,5},{7,6},{8,7},{9,8},{10,9... | collective-permute-start | bytes 86024 | tf_op jit(solution)/shard_map/ppermute | solution.py:83
  32.3 4.3 %copy-start.4 = (bf16[8,1792]{0,1:T(8,128)(2,1)}, bf16[8,1792]{0,1:T(8,128)(2,1)S(1)}, u32[]{:S(2)}) copy-start(bf16[8,1792]{0,1:T(8,128)(2,1)S(1)} %collective-permute-done.2) | copy-start | bytes 86020
  32.3 9.5 %collective-permute-start.4 = (bf16[8,1792]{0,1:T(8,128)(2,1)S(1)}, bf16[8,1792]{0,1:T(8,128)(2,1)S(1)}, u32[]{:S(2)}, u32[]{:S(2)}) collective-permute-start(bf16[8,1792]{0,1:T(8,128)(2,1)S(1)} %collective-permute-done.2), channel_id=1, source_target_pairs={{0,1},{1,2},{2,3},{3,4},{4,5},{5,6},{6,7},{7,8},{8,9},{9,10},{10,1... | collective-permute-start | bytes 86024 | tf_op jit(solution)/shard_map/ppermute | solution.py:80
  36.6 5.2 %copy-start.5 = (bf16[8,1792]{0,1:T(8,128)(2,1)}, bf16[8,1792]{0,1:T(8,128)(2,1)S(1)}, u32[]{:S(2)}) copy-start(bf16[8,1792]{0,1:T(8,128)(2,1)S(1)} %collective-permute-done.3) | copy-start | bytes 86020
  36.6 16.9 %collective-permute-start.5 = (bf16[8,1792]{0,1:T(8,128)(2,1)S(1)}, bf16[8,1792]{0,1:T(8,128)(2,1)}, u32[]{:S(2)}, u32[]{:S(2)}) collective-permute-start(bf16[8,1792]{0,1:T(8,128)(2,1)S(1)} %collective-permute-done.3), channel_id=1, source_target_pairs={{0,15},{1,0},{2,1},{3,2},{4,3},{5,4},{6,5},{7,6},{8,7},{9,8},{10,9... | collective-permute-start | bytes 86024 | tf_op jit(solution)/shard_map/ppermute | solution.py:83
  41.9 11.7 %copy-start.6 = (bf16[8,1792]{0,1:T(8,128)(2,1)}, bf16[8,1792]{0,1:T(8,128)(2,1)S(1)}, u32[]{:S(2)}) copy-start(bf16[8,1792]{0,1:T(8,128)(2,1)S(1)} %collective-permute-done.4) | copy-start | bytes 86020
  41.9 23.4 %collective-permute-start.6 = (bf16[8,1792]{0,1:T(8,128)(2,1)S(1)}, bf16[8,1792]{0,1:T(8,128)(2,1)}, u32[]{:S(2)}, u32[]{:S(2)}) collective-permute-start(bf16[8,1792]{0,1:T(8,128)(2,1)S(1)} %collective-permute-done.4), channel_id=1, source_target_pairs={{0,1},{1,2},{2,3},{3,4},{4,5},{5,6},{6,7},{7,8},{8,9},{9,10},{10,1... | collective-permute-start | bytes 86024 | tf_op jit(solution)/shard_map/ppermute | solution.py:80
  53.6 25.8 %collective-permute-start.7 = (bf16[8,1792]{0,1:T(8,128)(2,1)}, bf16[8,1792]{0,1:T(8,128)(2,1)}, u32[]{:S(2)}, u32[]{:S(2)}) collective-permute-start(bf16[8,1792]{0,1:T(8,128)(2,1)} %collective-permute-done.5), channel_id=1, source_target_pairs={{0,15},{1,0},{2,1},{3,2},{4,3},{5,4},{6,5},{7,6},{8,7},{9,8},{10,9... | collective-permute-start | bytes 86024 | tf_op jit(solution)/shard_map/ppermute | solution.py:83
  65.2 15.7 %collective-permute-start.8 = (bf16[8,1792]{0,1:T(8,128)(2,1)}, bf16[8,1792]{0,1:T(8,128)(2,1)}, u32[]{:S(2)}, u32[]{:S(2)}) collective-permute-start(bf16[8,1792]{0,1:T(8,128)(2,1)} %collective-permute-done.6), channel_id=1, source_target_pairs={{0,1},{1,2},{2,3},{3,4},{4,5},{5,6},{6,7},{7,8},{8,9},{9,10},{10,1... | collective-permute-start | bytes 86024 | tf_op jit(solution)/shard_map/ppermute | solution.py:80
  79.4 11.0 %collective-permute-start.9 = (bf16[8,1792]{0,1:T(8,128)(2,1)}, bf16[8,1792]{0,1:T(8,128)(2,1)}, u32[]{:S(2)}, u32[]{:S(2)}) collective-permute-start(bf16[8,1792]{0,1:T(8,128)(2,1)} %collective-permute-done.7), channel_id=1, source_target_pairs={{0,15},{1,0},{2,1},{3,2},{4,3},{5,4},{6,5},{7,6},{8,7},{9,8},{10,9... | collective-permute-start | bytes 86024 | tf_op jit(solution)/shard_map/ppermute | solution.py:83
  81.0 9.6 %collective-permute-start.10 = (bf16[8,1792]{0,1:T(8,128)(2,1)}, bf16[8,1792]{0,1:T(8,128)(2,1)}, u32[]{:S(2)}, u32[]{:S(2)}) collective-permute-start(bf16[8,1792]{0,1:T(8,128)(2,1)} %collective-permute-done.8), channel_id=1, source_target_pairs={{0,1},{1,2},{2,3},{3,4},{4,5},{5,6},{6,7},{7,8},{8,9},{9,10},{10,1... | collective-permute-start | bytes 86024 | tf_op jit(solution)/shard_map/ppermute | solution.py:80
  90.3 14.0 %collective-permute-start.11 = (bf16[8,1792]{0,1:T(8,128)(2,1)}, bf16[8,1792]{0,1:T(8,128)(2,1)}, u32[]{:S(2)}, u32[]{:S(2)}) collective-permute-start(bf16[8,1792]{0,1:T(8,128)(2,1)} %collective-permute-done.9), channel_id=1, source_target_pairs={{0,15},{1,0},{2,1},{3,2},{4,3},{5,4},{6,5},{7,6},{8,7},{9,8},{10,9... | collective-permute-start | bytes 86024 | tf_op jit(solution)/shard_map/ppermute | solution.py:83
  90.5 13.8 %collective-permute-start.12 = (bf16[8,1792]{0,1:T(8,128)(2,1)}, bf16[8,1792]{0,1:T(8,128)(2,1)}, u32[]{:S(2)}, u32[]{:S(2)}) collective-permute-start(bf16[8,1792]{0,1:T(8,128)(2,1)} %collective-permute-done.10), channel_id=1, source_target_pairs={{0,1},{1,2},{2,3},{3,4},{4,5},{5,6},{6,7},{7,8},{8,9},{9,10},{10,1... | collective-permute-start | bytes 86024 | tf_op jit(solution)/shard_map/ppermute | solution.py:80
  104.3 86.3 %collective-permute-start.13 = (bf16[8,1792]{0,1:T(8,128)(2,1)}, bf16[8,1792]{0,1:T(8,128)(2,1)}, u32[]{:S(2)}, u32[]{:S(2)}) collective-permute-start(bf16[8,1792]{0,1:T(8,128)(2,1)} %collective-permute-done.11), channel_id=1, source_target_pairs={{0,15},{1,0},{2,1},{3,2},{4,3},{5,4},{6,5},{7,6},{8,7},{9,8},{10,9... | collective-permute-start | bytes 86024 | tf_op jit(solution)/shard_map/ppermute | solution.py:83
  104.3 92.3 %collective-permute-start.14 = (bf16[8,1792]{0,1:T(8,128)(2,1)}, bf16[8,1792]{0,1:T(8,128)(2,1)}, u32[]{:S(2)}, u32[]{:S(2)}) collective-permute-start(bf16[8,1792]{0,1:T(8,128)(2,1)} %collective-permute-done.12), channel_id=1, source_target_pairs={{0,1},{1,2},{2,3},{3,4},{4,5},{5,6},{6,7},{7,8},{8,9},{9,10},{10,1... | collective-permute-start | bytes 86024 | tf_op jit(solution)/shard_map/ppermute | solution.py:80
  205.2 3.0 %copy-start.1 = (f32[2,1024,128,7]{2,1,3,0:T(8,128)}, f32[2,1024,128,7]{2,1,3,0:T(8,128)S(1)}, u32[]{:S(2)}) copy-start(f32[2,1024,128,7]{2,1,3,0:T(8,128)S(1)} %get-tuple-element.38) | copy-start | bytes 22020100
  210.9 18.2 %all-to-all-start.2 = ((f32[1,128,14]{2,0,1:T(1,128)}), f32[1,128,14]{2,0,1:T(1,128)S(1)}, u32[]{:S(2)}, u32[]{:S(2)}) async-start(f32[1,128,14]{2,0,1:T(1,128)} %copy.28), calls=%async_computation.2 | async-start | bytes 131072 | tf_op jit(solution)/shard_map/all_to_all | solution.py:113
  229.0 12.0 %all-to-all-start.1 = ((f32[1,128,14]{2,0,1:T(1,128)}), f32[1,128,14]{2,0,1:T(1,128)S(1)}, u32[]{:S(2)}, u32[]{:S(2)}) async-start(f32[1,128,14]{2,0,1:T(1,128)} %copy.25), calls=%async_computation.1 | async-start | bytes 131072 | tf_op jit(solution)/shard_map/all_to_all | solution.py:106
  241.0 28.3 %all-to-all-start = ((f32[1,128,1792]{2,0,1:T(1,128)}), f32[1,128,1792]{2,0,1:T(1,128)S(1)}, u32[]{:S(2)}, u32[]{:S(2)}) async-start(f32[1,128,1792]{2,0,1:T(1,128)} %copy.24), calls=%async_computation | async-start | bytes 1835008 | tf_op jit(solution)/shard_map/all_to_all | solution.py:99
Sparse Core Ops, SparseCore 0:
  9.6 89.0 all-gather.1
